TPU v7x, 512 devices: a whole 4x4x16 slice. The times are simulated.
512 devices in a mesh: rows: 64 (over y, z), cols: 8 (over x, core).
Axes of the slice: x: 4, y: 4, z: 16, core: 2. Of those that a mesh axis runs over, the one named last changes fastest.
Arguments:
- node_features: bfloat16 [65536, 512], P('rows', 'cols'), may hold values from -6 to 6
- weight: bfloat16 [512, 512], replicated, may hold values from -0.25 to 0.25
- tile_values: bfloat16 [4096, 128, 128], P('rows'), may hold values from -0.1875 to 0.1875
- tile_row: int32 [4096], P('rows'), may hold values from 0 to 7
- source_owner: int32 [4096, 1], P('rows'), may hold values from 0 to 63; in each aligned block of 64 rows (0 to 63, 64 to 127, ...) at most 2 rows name the same one
- source_block: int32 [4096], P('rows'), may hold values from 0 to 7
- labels: int32 [65536], P('rows'), may hold values from 0 to 511
Outputs:
- activations: bfloat16 [65536, 512], P('rows', 'cols')
- weight_grad: float32 [512, 512], P(None, 'cols')
- feature_grad: bfloat16 [65536, 512], P('rows', 'cols')
Inputs may be any that keep to these rules, and one draw needn't show every extreme that they name: `source_owner`: of the 64 tiles of one index of rows, at most 2 name the same owner.
All inputs are finite; a program needn't handle non-finite values.
Results may differ from a plain program's by a relative error of at most 0.0095.
Values may be sent and summed in bfloat16 or wider, within the bound.
A program may use at most 64 MiB of HBM per device.

v0:
```python
import math
import jax
import jax.numpy as jnp
from jax import lax
from jax.sharding import PartitionSpec as P


def slot_ranks(owners):
    positions = jnp.arange(owners.shape[0], dtype=jnp.int32)
    earlier = (owners[:, None] == owners[None, :]) & (positions[None, :] < positions[:, None])
    return jnp.sum(earlier.astype(jnp.int32), axis=1)


def rows_exchange(x):
    return lax.all_to_all(x, "rows", split_axis=0, concat_axis=0, tiled=True)


def row_all_reduce(partial):
    row_devices = lax.axis_size("rows")
    k, c = partial.shape
    pieces = partial.reshape(row_devices, k // row_devices, c)
    reduced = jnp.sum(rows_exchange(pieces), axis=0)
    return lax.all_gather(reduced, "rows", axis=0, tiled=True)


def per_device(node_features, weight, tile_values, tile_row, source_owner, source_block, labels):
    local_rows, col_width = node_features.shape
    block_size = tile_values.shape[1]
    local_blocks = local_rows // block_size
    row_devices = lax.axis_size("rows")
    col_devices = lax.axis_size("cols")
    tiles = tile_values.shape[0]
    capacity = 2 * tiles // row_devices
    half = col_width // 2
    owners = source_owner[:, 0]
    slot_rank = slot_ranks(owners)
    local_ids = jnp.arange(local_blocks, dtype=jnp.int32)
    row_onehot = (tile_row[:, None] == local_ids[None, :]).astype(jnp.float32)
    tile_ids = jnp.arange(tiles, dtype=jnp.int32)
    in_slot = (owners[:, None, None] == jnp.arange(row_devices, dtype=jnp.int32)[None, :, None]) & (
        slot_rank[:, None, None] == jnp.arange(capacity, dtype=jnp.int32)[None, None, :]
    )
    request = jnp.sum(jnp.where(in_slot, source_block[:, None, None], 0), axis=0)
    slot_tile = jnp.sum(jnp.where(in_slot, tile_ids[:, None, None] - tiles, 0), axis=0) + tiles
    wanted = rows_exchange(request)
    own_blocks = node_features.reshape(local_blocks, block_size, col_width)
    outgoing = own_blocks[wanted]
    col_index = lax.axis_index("cols")
    w_columns = lax.dynamic_slice_in_dim(weight, col_index * col_width, col_width, 1)
    w_rows = lax.dynamic_slice_in_dim(weight, col_index * col_width, col_width, 0)
    w_split = w_columns.reshape(col_devices, col_width, col_width)

    def aggregate(part):
        source_rows = part[owners, slot_rank]
        products = jnp.einsum(
            "tij,tjf->tif", tile_values, source_rows, preferred_element_type=jnp.float32
        )
        summed = jnp.einsum("tb,tif->bif", row_onehot, products, precision=lax.Precision.HIGHEST)
        return summed.reshape(local_rows, part.shape[-1]).astype(jnp.bfloat16)

    first = aggregate(rows_exchange(outgoing[..., :half]))
    second_out, first = lax.optimization_barrier((outgoing[..., half:], first))
    first_all = lax.all_gather(first, "cols", axis=0, tiled=False)
    second = aggregate(rows_exchange(second_out))
    second_all = lax.all_gather(second, "cols", axis=0, tiled=False)
    hidden = jnp.einsum(
        "jnf,jfc->nc", first_all, w_split[:, :half], preferred_element_type=jnp.float32
    ) + jnp.einsum("jnf,jfc->nc", second_all, w_split[:, half:], preferred_element_type=jnp.float32)
    sigmoid = jax.nn.sigmoid(hidden)
    activated = hidden * sigmoid
    slopes = sigmoid * (1.0 + hidden * (1.0 - sigmoid))
    feature_ids = col_index * col_width + jnp.arange(col_width, dtype=jnp.int32)
    target = (labels[:, None] == feature_ids[None, :]).astype(jnp.float32)
    out_grad = ((activated - target) * slopes).astype(jnp.bfloat16)
    grad_all = lax.all_gather(out_grad, "cols", axis=1, tiled=True)
    weight_terms = jnp.concatenate(
        [
            jnp.einsum("jnf,nc->jfc", first_all, out_grad, preferred_element_type=jnp.float32),
            jnp.einsum("jnf,nc->jfc", second_all, out_grad, preferred_element_type=jnp.float32),
        ],
        axis=1,
    ).reshape(col_devices * col_width, col_width)
    node_total = local_rows * row_devices
    weight_grad = row_all_reduce(weight_terms) / math.sqrt(node_total)
    agg_grad = jnp.einsum("nc,kc->nk", grad_all, w_rows, preferred_element_type=jnp.float32).astype(
        jnp.bfloat16
    )
    grad_rows = agg_grad.reshape(local_blocks, block_size, col_width)[tile_row]
    sent_terms = jnp.einsum(
        "tji,tjf->tif", tile_values, grad_rows, preferred_element_type=jnp.float32
    ).astype(jnp.bfloat16)
    padded_terms = jnp.concatenate([sent_terms, jnp.zeros_like(sent_terms[:1])], axis=0)
    received = rows_exchange(padded_terms[slot_tile])
    placing = (wanted[:, :, None] == local_ids[None, None, :]).astype(jnp.float32)
    feature_grad = jnp.einsum(
        "scb,scif->bif", placing, received.astype(jnp.float32), precision=lax.Precision.HIGHEST
    ).reshape(local_rows, col_width)
    return (activated.astype(jnp.bfloat16), weight_grad, feature_grad.astype(jnp.bfloat16))


def solution(mesh):
    return jax.shard_map(
        per_device,
        mesh=mesh,
        in_specs=(
            P("rows", "cols"),
            P(),
            P("rows", None, None),
            P("rows"),
            P("rows", None),
            P("rows"),
            P("rows"),
        ),
        out_specs=(P("rows", "cols"), P(None, "cols"), P("rows", "cols")),
        check_vma=False,
    )
```

profile of v0, /device:TPU:8, one launch (start us, length us, event | category | flops | bytes accessed | tf_op | source)
XLA Modules:
  0.0 418.3 jit_solution(6826741657737070376)
XLA Ops:
  7.2 1.0 convert_reduce_fusion
  10.4 18.7 %all-to-all-start = ((s32[64,1,2]{2,1,0:T(1,128)}), s32[64,1,2]{2,1,0:T(1,128)S(1)}, u32[]{:S(2)}, u32[]{:S(2)}) async-start(s32[64,1,2]{2,1,0:T(1,128)} %copy.57), calls=%async_computation | async-start | bytes 65536 | tf_op jit(solution)/shard_map/all_to_all | solution.py:15
  29.2 0.9 copy_bitcast_fusion.2
  30.1 12.5 %all-to-all-done = s32[64,1,2]{2,1,0:T(1,128)S(1)} async-done(((s32[64,1,2]{2,1,0:T(1,128)}), s32[64,1,2]{2,1,0:T(1,128)S(1)}, u32[]{:S(2)}, u32[]{:S(2)}) %all-to-all-start) | async-done | bytes 544 | tf_op jit(solution)/shard_map/all_to_all | solution.py:15
  43.0 2.2 gather_fusion
  45.1 3.3 fusion.40
  48.4 6.5 %all-to-all-start.1 = ((bf16[64,2,128,32]{2,3,1,0:T(8,128)(2,1)}), bf16[64,2,128,32]{2,3,1,0:T(8,128)(2,1)}, u32[]{:S(2)}, u32[]{:S(2)}) async-start(bf16[64,2,128,32]{2,3,1,0:T(8,128)(2,1)} %get-tuple-element.15), calls=%async_computation.1 | async-start | bytes 2097152 | tf_op jit(solution)/shard_map/all_to_all | solution.py:15
  54.9 52.2 %all-to-all-done.1 = bf16[64,2,128,32]{2,3,1,0:T(8,128)(2,1)} async-done(((bf16[64,2,128,32]{2,3,1,0:T(8,128)(2,1)}), bf16[64,2,128,32]{2,3,1,0:T(8,128)(2,1)}, u32[]{:S(2)}, u32[]{:S(2)}) %all-to-all-start.1) | async-done | bytes 1048608 | tf_op jit(solution)/shard_map/all_to_all | solution.py:15
  107.1 2.0 gather_fusion.1
  109.0 1.2 convolution_bitcast_fusion.1
  110.2 1.1 convolution_convert_fusion.3
  111.3 7.4 %all-to-all-start.2 = ((bf16[64,2,128,32]{2,3,1,0:T(8,128)(2,1)}), bf16[64,2,128,32]{2,3,1,0:T(8,128)(2,1)}, u32[]{:S(2)}, u32[]{:S(2)}) async-start(bf16[64,2,128,32]{2,3,1,0:T(8,128)(2,1)} %get-tuple-element.6), calls=%async_computation.2 | async-start | bytes 2097152 | tf_op jit(solution)/shard_map/all_to_all | solution.py:15
  118.8 1.0 constant_dynamic-slice_fusion
  119.9 13.5 %all-gather = bf16[8192,32]{0,1:T(8,128)(2,1)S(1)} all-gather(bf16[1024,32]{0,1:T(8,128)(2,1)S(1)} %bitcast.101), channel_id=2, replica_groups=mesh['rows'=64,'cols'=8] {'cols'}, dimensions={0}, use_global_device_ids=true | all-gather | bytes 589824 | tf_op jit(solution)/shard_map/all_gather | solution.py:63
  133.6 38.6 %all-to-all-done.2 = bf16[64,2,128,32]{2,3,1,0:T(8,128)(2,1)} async-done(((bf16[64,2,128,32]{2,3,1,0:T(8,128)(2,1)}), bf16[64,2,128,32]{2,3,1,0:T(8,128)(2,1)}, u32[]{:S(2)}, u32[]{:S(2)}) %all-to-all-start.2) | async-done | bytes 1048608 | tf_op jit(solution)/shard_map/all_to_all | solution.py:15
  172.2 2.0 gather_fusion.2
  174.1 1.2 convolution_bitcast_fusion
  175.3 1.1 convolution_convert_fusion.2
  176.4 13.5 %all_gather.18 = bf16[8,1024,32]{1,2,0:T(8,128)(2,1)S(1)} all-gather(bf16[1,1024,32]{1,2,0:T(8,128)(2,1)S(1)} %convert_element_type.53), channel_id=1, replica_groups=mesh['rows'=64,'cols'=8] {'cols'}, dimensions={0}, use_global_device_ids=true | all-gather | bytes 589824 | tf_op jit(solution)/shard_map/all_gather | solution.py:65
  190.2 1.0 multiply_convert_fusion
  191.5 1.2 fusion.15
  192.8 1.2 fusion.17
  194.1 0.8 reshape.206
  194.9 6.9 %all-to-all-start.3 = ((f32[64,1,512]{2,1,0:T(1,128)}), f32[64,1,512]{2,1,0:T(1,128)S(1)}, u32[]{:S(2)}, u32[]{:S(2)}) async-start(f32[64,1,512]{2,1,0:T(1,128)} %reshape.206), calls=%async_computation.3 | async-start | bytes 262144 | tf_op jit(solution)/shard_map/all_to_all | solution.py:15
  201.8 12.5 %all-gather.3.cloned.1.call-done = bf16[1024,512]{0,1:T(8,128)(2,1)} async-done(((bf16[1024,64]{0,1:T(8,128)(2,1)}), bf16[1024,512]{0,1:T(8,128)(2,1)}) %all-gather.3.cloned.1.call-update) | async-done | bytes 1048592 | tf_op jit(solution)/shard_map/all_gather | solution.py:75
  214.3 1.6 fusion.10
  217.4 2.1 gather_fusion.4
  219.5 5.1 %copy.71 = bf16[64,2,128,64]{2,1,3,0:T(2,128)(2,1)} copy(bf16[64,2,128,64]{2,3,1,0:T(8,128)(2,1)} %bitcast.93) | data formatting | bytes 4194304 | tf_op jit(solution)/shard_map/gather | solution.py:93
  224.6 15.9 %all-to-all-start.4 = ((bf16[64,2,128,64]{2,1,3,0:T(2,128)(2,1)}), bf16[64,2,128,64]{2,1,3,0:T(2,128)(2,1)}, u32[]{:S(2)}, u32[]{:S(2)}) async-start(bf16[64,2,128,64]{2,1,3,0:T(2,128)(2,1)} %copy.71), calls=%async_computation.4 | async-start | bytes 4194304 | tf_op jit(solution)/shard_map/all_to_all | solution.py:15
  241.1 0.9 reduce
  242.2 163.9 %all_gather.19 = f32[512,64]{1,0:T(8,128)S(1)} all-gather(f32[8,64]{1,0:T(8,128)S(1)} %reduce_sum.41), channel_id=1, replica_groups=mesh['rows'=64,'cols'=8] {'rows'}, dimensions={0}, use_global_device_ids=true | all-gather | bytes 133120 | tf_op jit(solution)/shard_map/all_gather | solution.py:23
  406.9 3.9 fusion.7
  (48 shorter events, 7.3 us)
Async XLA Ops:
  7.2 101.9 %copy-start = (bf16[64,128,128]{2,1,0:T(8,128)(2,1)S(1)}, bf16[64,128,128]{2,1,0:T(8,128)(2,1)}, u32[]{:S(2)}) copy-start(bf16[64,128,128]{2,1,0:T(8,128)(2,1)} %param.9) | copy-start | bytes 6291460
  10.4 32.2 %all-to-all-start = ((s32[64,1,2]{2,1,0:T(1,128)}), s32[64,1,2]{2,1,0:T(1,128)S(1)}, u32[]{:S(2)}, u32[]{:S(2)}) async-start(s32[64,1,2]{2,1,0:T(1,128)} %copy.57), calls=%async_computation | async-start | bytes 65536 | tf_op jit(solution)/shard_map/all_to_all | solution.py:15
  48.4 6.5 %copy-start.2 = (s32[64,1]{0,1:T(1,128)S(1)}, s32[64,1]{0,1:T(1,128)}, u32[]{:S(2)}) copy-start(s32[64,1]{0,1:T(1,128)} %param.11) | copy-start | bytes 772
  48.4 58.7 %all-to-all-start.1 = ((bf16[64,2,128,32]{2,3,1,0:T(8,128)(2,1)}), bf16[64,2,128,32]{2,3,1,0:T(8,128)(2,1)}, u32[]{:S(2)}, u32[]{:S(2)}) async-start(bf16[64,2,128,32]{2,3,1,0:T(8,128)(2,1)} %get-tuple-element.15), calls=%async_computation.1 | async-start | bytes 2097152 | tf_op jit(solution)/shard_map/all_to_all | solution.py:15
  109.0 1.2 copy-start.1
  111.3 60.9 %all-to-all-start.2 = ((bf16[64,2,128,32]{2,3,1,0:T(8,128)(2,1)}), bf16[64,2,128,32]{2,3,1,0:T(8,128)(2,1)}, u32[]{:S(2)}, u32[]{:S(2)}) async-start(bf16[64,2,128,32]{2,3,1,0:T(8,128)(2,1)} %get-tuple-element.6), calls=%async_computation.2 | async-start | bytes 2097152 | tf_op jit(solution)/shard_map/all_to_all | solution.py:15
  118.8 95.5 %all-gather.3.cloned.1.call-start = ((), (), s32[]{:S(2)}) async-start(), calls=%async_computation.5 | async-start | bytes 1179648 | tf_op jit(solution)/shard_map/all_gather | solution.py:75
  175.3 14.8 %copy-start.3 = (s32[1024]{0:T(1024)S(1)}, s32[1024]{0:T(1024)}, u32[]{:S(2)}) copy-start(s32[1024]{0:T(1024)} %param.13) | copy-start | bytes 12292
  194.9 29.7 %all-to-all-start.3 = ((f32[64,1,512]{2,1,0:T(1,128)}), f32[64,1,512]{2,1,0:T(1,128)S(1)}, u32[]{:S(2)}, u32[]{:S(2)}) async-start(f32[64,1,512]{2,1,0:T(1,128)} %reshape.206), calls=%async_computation.3 | async-start | bytes 262144 | tf_op jit(solution)/shard_map/all_to_all | solution.py:15
  224.6 182.2 %all-to-all-start.4 = ((bf16[64,2,128,64]{2,1,3,0:T(2,128)(2,1)}), bf16[64,2,128,64]{2,1,3,0:T(2,128)(2,1)}, u32[]{:S(2)}, u32[]{:S(2)}) async-start(bf16[64,2,128,64]{2,1,3,0:T(2,128)(2,1)} %copy.71), calls=%async_computation.4 | async-start | bytes 4194304 | tf_op jit(solution)/shard_map/all_to_all | solution.py:15
Sparse Core Ops, SparseCore 0:
  191.3 22.9 all-gather.2
where the time goes:
time: 419 us; the launch traced here: 418 us
  blocking collectives  191 us (46%)
  waiting for transfers between devices  116 us (28%)
  starting transfers between devices  55.5 us (13%)
  local copies, waits for them, and re-layouts  24 us (6%)
  between operations  14.4 us (3%)
  matrix products  14.3 us (3%)
    all_gather x1, blocking collectives, row_all_reduce(): return lax.all_gather(reduced, 'rows', axis=0, tiled=True)  164 us
    all_to_all x5, waiting for transfers between devices, rows_exchange(): return lax.all_to_all(x, 'rows', split_axis=0, concat_axis=0, tiled=True)  103 us
    all_to_all x5, starting transfers between devices, rows_exchange(): return lax.all_to_all(x, 'rows', split_axis=0, concat_axis=0, tiled=True)  55.4 us
    all_gather x1, blocking collectives, per_device(): first_all = lax.all_gather(first, 'cols', axis=0, tiled=False)  13.5 us
    all_gather x1, blocking collectives, per_device(): second_all = lax.all_gather(second, 'cols', axis=0, tiled=False)  13.5 us
    all_gather x1, waiting for transfers between devices, per_device(): grad_all = lax.all_gather(out_grad, 'cols', axis=1, tiled=True)  12.5 us
  transfers between devices with their start and end apart: 6, of which 4 were waited for; matrix products, arithmetic and copies ran while one was open for 4% of the time, Pallas kernels for 0%

commit v1 on v0

--- a/solution.py
+++ b/solution.py
@@ -1,8 +1,18 @@
+import functools
 import math
 import jax
 import jax.numpy as jnp
 from jax import lax
 from jax.sharding import PartitionSpec as P
+
+
+def find_tasks(point, comm_axis, along_dim):
+    u_next = jnp.stack([point] * lax.axis_size(comm_axis), axis=0)
+    y1 = lax.all_to_all(u_next, comm_axis, 0, 0)
+    return jnp.concatenate(y1, axis=along_dim)
+
+
+process_counts = functools.partial(find_tasks, comm_axis="rows", along_dim=0)
 
 
 def slot_ranks(owners):
@@ -20,7 +30,7 @@
     k, c = partial.shape
     pieces = partial.reshape(row_devices, k // row_devices, c)
     reduced = jnp.sum(rows_exchange(pieces), axis=0)
-    return lax.all_gather(reduced, "rows", axis=0, tiled=True)
+    return process_counts(reduced)
 
 
 def per_device(node_features, weight, tile_values, tile_row, source_owner, source_block, labels):

time: 419 us -> 362 us (0.86)
  blocking collectives: 191 us -> 26.9 us
  waiting for transfers between devices: 116 us -> 220 us
    all_gather x1 -> x0, blocking collectives: 164 us -> none  [row_all_reduce(): return lax.all_gather(reduced, 'rows', axis=0, tiled=True)]
    all_to_all x5, waiting for transfers between devices: 103 us -> 215 us  [rows_exchange(): return lax.all_to_all(x, 'rows', split_axis=0, concat_axis=0, tiled=True)]
    all_gather x1, waiting for transfers between devices: 12.5 us -> 0.02 us  [per_device(): grad_all = lax.all_gather(out_grad, 'cols', axis=1, tiled=True)]
    all_to_all x0 -> x1, starting transfers between devices: none -> 6.25 us  [find_tasks(): y1 = lax.all_to_all(u_next, comm_axis, 0, 0)]
    all_to_all x5, starting transfers between devices: 55.4 us -> 49.8 us  [rows_exchange(): return lax.all_to_all(x, 'rows', split_axis=0, concat_axis=0, tiled=True)]
    all_to_all x0 -> x1, waiting for transfers between devices: none -> 5.04 us  [find_tasks(): y1 = lax.all_to_all(u_next, comm_axis, 0, 0)]
  transfers between devices with their start and end apart: 6 -> 7, of which waited for: 4 -> 6; matrix products, arithmetic and copies ran while one was open for 4% -> 6% of each run, Pallas kernels for 0% -> 0%
where the time goes in v1:
time: 362 us; the launch traced here: 361 us
  waiting for transfers between devices  220 us (61%)
  starting transfers between devices  56.1 us (15%)
  blocking collectives  26.9 us (7%)
  local copies, waits for them, and re-layouts  25 us (7%)
  between operations  14.4 us (4%)
  matrix products  14.3 us (4%)
  other arithmetic  4.64 us (1%)
    all_to_all x5, waiting for transfers between devices, rows_exchange(): return lax.all_to_all(x, 'rows', split_axis=0, concat_axis=0, tiled=True)  215 us
    all_to_all x5, starting transfers between devices, rows_exchange(): return lax.all_to_all(x, 'rows', split_axis=0, concat_axis=0, tiled=True)  49.8 us
    all_gather x1, blocking collectives, per_device(): first_all = lax.all_gather(first, 'cols', axis=0, tiled=False)  13.5 us
    all_gather x1, blocking collectives, per_device(): second_all = lax.all_gather(second, 'cols', axis=0, tiled=False)  13.5 us
  transfers between devices with their start and end apart: 7, of which 6 were waited for; matrix products, arithmetic and copies ran while one was open for 6% of the time, Pallas kernels for 0%

profile of v1, /device:TPU:8, one launch (start us, length us, event | category | flops | bytes accessed | tf_op | source)
XLA Modules:
  0.0 361.1 jit_solution(18230123403996624552)
XLA Ops:
  7.2 1.0 convert_reduce_fusion
  10.4 18.7 %all-to-all-start = ((s32[64,1,2]{2,1,0:T(1,128)}), s32[64,1,2]{2,1,0:T(1,128)S(1)}, u32[]{:S(2)}, u32[]{:S(2)}) async-start(s32[64,1,2]{2,1,0:T(1,128)} %copy.60), calls=%async_computation | async-start | bytes 65536 | tf_op jit(solution)/shard_map/all_to_all | solution.py:25
  30.1 12.5 %all-to-all-done = s32[64,1,2]{2,1,0:T(1,128)S(1)} async-done(((s32[64,1,2]{2,1,0:T(1,128)}), s32[64,1,2]{2,1,0:T(1,128)S(1)}, u32[]{:S(2)}, u32[]{:S(2)}) %all-to-all-start) | async-done | bytes 544 | tf_op jit(solution)/shard_map/all_to_all | solution.py:25
  43.0 2.1 gather_fusion
  45.1 3.3 fusion.40
  48.4 6.5 %all-to-all-start.1 = ((bf16[64,2,128,32]{2,3,1,0:T(8,128)(2,1)}), bf16[64,2,128,32]{2,3,1,0:T(8,128)(2,1)}, u32[]{:S(2)}, u32[]{:S(2)}) async-start(bf16[64,2,128,32]{2,3,1,0:T(8,128)(2,1)} %get-tuple-element.24), calls=%async_computation.1 | async-start | bytes 2097152 | tf_op jit(solution)/shard_map/all_to_all | solution.py:25
  54.9 52.2 %all-to-all-done.1 = bf16[64,2,128,32]{2,3,1,0:T(8,128)(2,1)} async-done(((bf16[64,2,128,32]{2,3,1,0:T(8,128)(2,1)}), bf16[64,2,128,32]{2,3,1,0:T(8,128)(2,1)}, u32[]{:S(2)}, u32[]{:S(2)}) %all-to-all-start.1) | async-done | bytes 1048608 | tf_op jit(solution)/shard_map/all_to_all | solution.py:25
  107.1 2.0 gather_fusion.1
  109.0 1.2 convolution_bitcast_fusion.1
  110.2 1.1 convolution_convert_fusion.3
  111.3 7.4 %all-to-all-start.2 = ((bf16[64,2,128,32]{2,3,1,0:T(8,128)(2,1)}), bf16[64,2,128,32]{2,3,1,0:T(8,128)(2,1)}, u32[]{:S(2)}, u32[]{:S(2)}) async-start(bf16[64,2,128,32]{2,3,1,0:T(8,128)(2,1)} %get-tuple-element.6), calls=%async_computation.2 | async-start | bytes 2097152 | tf_op jit(solution)/shard_map/all_to_all | solution.py:25
  118.8 1.0 constant_dynamic-slice_fusion
  119.9 13.5 %all-gather = bf16[8192,32]{0,1:T(8,128)(2,1)S(1)} all-gather(bf16[1024,32]{0,1:T(8,128)(2,1)S(1)} %bitcast.103), channel_id=2, replica_groups=mesh['rows'=64,'cols'=8] {'cols'}, dimensions={0}, use_global_device_ids=true | all-gather | bytes 589824 | tf_op jit(solution)/shard_map/all_gather | solution.py:73
  133.6 38.6 %all-to-all-done.2 = bf16[64,2,128,32]{2,3,1,0:T(8,128)(2,1)} async-done(((bf16[64,2,128,32]{2,3,1,0:T(8,128)(2,1)}), bf16[64,2,128,32]{2,3,1,0:T(8,128)(2,1)}, u32[]{:S(2)}, u32[]{:S(2)}) %all-to-all-start.2) | async-done | bytes 1048608 | tf_op jit(solution)/shard_map/all_to_all | solution.py:25
  172.2 2.0 gather_fusion.2
  174.1 1.2 convolution_bitcast_fusion
  175.3 1.1 convolution_convert_fusion.2
  176.4 13.5 %all_gather.15 = bf16[8,1024,32]{1,2,0:T(8,128)(2,1)S(1)} all-gather(bf16[1,1024,32]{1,2,0:T(8,128)(2,1)S(1)} %convert_element_type.53), channel_id=1, replica_groups=mesh['rows'=64,'cols'=8] {'cols'}, dimensions={0}, use_global_device_ids=true | all-gather | bytes 589824 | tf_op jit(solution)/shard_map/all_gather | solution.py:75
  190.2 1.0 multiply_convert_fusion
  191.2 1.2 fusion.15
  192.5 1.2 fusion.17
  194.6 6.9 %all-to-all-start.3 = ((f32[64,1,512]{2,1,0:T(1,128)}), f32[64,1,512]{2,1,0:T(1,128)S(1)}, u32[]{:S(2)}, u32[]{:S(2)}) async-start(f32[64,1,512]{2,1,0:T(1,128)} %reshape.211), calls=%async_computation.3 | async-start | bytes 262144 | tf_op jit(solution)/shard_map/all_to_all | solution.py:25
  201.8 15.9 %all-to-all-done.3 = f32[64,1,512]{2,1,0:T(1,128)S(1)} async-done(((f32[64,1,512]{2,1,0:T(1,128)}), f32[64,1,512]{2,1,0:T(1,128)S(1)}, u32[]{:S(2)}, u32[]{:S(2)}) %all-to-all-start.3) | async-done | bytes 131104 | tf_op jit(solution)/shard_map/all_to_all | solution.py:25
  220.2 6.3 %all-to-all-start.4 = ((f32[64,1,512]{2,1,0:T(1,128)}), f32[64,1,512]{2,1,0:T(1,128)S(1)}, u32[]{:S(2)}, u32[]{:S(2)}) async-start(f32[64,1,512]{2,1,0:T(1,128)} %reshape.213), calls=%async_computation.4 | async-start | bytes 262144 | tf_op jit(solution)/shard_map/all_to_all | solution.py:11
  226.6 1.6 fusion.10
  229.7 2.1 gather_fusion.4
  231.8 5.1 %copy.74 = bf16[64,2,128,64]{2,1,3,0:T(2,128)(2,1)} copy(bf16[64,2,128,64]{2,3,1,0:T(8,128)(2,1)} %bitcast.95) | data formatting | bytes 4194304 | tf_op jit(solution)/shard_map/gather | solution.py:103
  236.9 5.0 %all-to-all-done.4 = f32[64,1,512]{2,1,0:T(1,128)S(1)} async-done(((f32[64,1,512]{2,1,0:T(1,128)}), f32[64,1,512]{2,1,0:T(1,128)S(1)}, u32[]{:S(2)}, u32[]{:S(2)}) %all-to-all-start.4) | async-done | bytes 131104 | tf_op jit(solution)/shard_map/all_to_all | solution.py:11
  241.9 10.3 %all-to-all-start.5 = ((bf16[64,2,128,64]{2,1,3,0:T(2,128)(2,1)}), bf16[64,2,128,64]{2,1,3,0:T(2,128)(2,1)}, u32[]{:S(2)}, u32[]{:S(2)}) async-start(bf16[64,2,128,64]{2,1,3,0:T(2,128)(2,1)} %copy.74), calls=%async_computation.5 | async-start | bytes 4194304 | tf_op jit(solution)/shard_map/all_to_all | solution.py:25
  252.2 1.0 reduce.1
  254.1 95.6 %all-to-all-done.5 = bf16[64,2,128,64]{2,1,3,0:T(2,128)(2,1)} async-done(((bf16[64,2,128,64]{2,1,3,0:T(2,128)(2,1)}), bf16[64,2,128,64]{2,1,3,0:T(2,128)(2,1)}, u32[]{:S(2)}, u32[]{:S(2)}) %all-to-all-start.5) | async-done | bytes 2097184 | tf_op jit(solution)/shard_map/all_to_all | solution.py:25
  349.7 3.9 %fusion.7 = bf16[8,128,64]{1,0,2:T(8,128)(2,1)S(1)} fusion(bf16[64,2,128,64]{2,1,3,0:T(2,128)(2,1)} %all-to-all-done.5, s32[64,2]{0,1:T(2,128)S(1)} %bitcast.106), kind=kOutput, calls=%fused_computation.15 | convolution fusion | flops 16843776 | bytes 2228736 | tf_op jit(solution)/shard_map/scb,scif->bif/dot_general | solution.py:105
  (53 shorter events, 11.1 us)
Async XLA Ops:
  7.2 101.9 %copy-start = (bf16[64,128,128]{2,1,0:T(8,128)(2,1)S(1)}, bf16[64,128,128]{2,1,0:T(8,128)(2,1)}, u32[]{:S(2)}) copy-start(bf16[64,128,128]{2,1,0:T(8,128)(2,1)} %param.9) | copy-start | bytes 6291460
  10.4 32.2 %all-to-all-start = ((s32[64,1,2]{2,1,0:T(1,128)}), s32[64,1,2]{2,1,0:T(1,128)S(1)}, u32[]{:S(2)}, u32[]{:S(2)}) async-start(s32[64,1,2]{2,1,0:T(1,128)} %copy.60), calls=%async_computation | async-start | bytes 65536 | tf_op jit(solution)/shard_map/all_to_all | solution.py:25
  48.4 6.5 %copy-start.2 = (s32[64,1]{0,1:T(1,128)S(1)}, s32[64,1]{0,1:T(1,128)}, u32[]{:S(2)}) copy-start(s32[64,1]{0,1:T(1,128)} %param.11) | copy-start | bytes 772
  48.4 58.7 %all-to-all-start.1 = ((bf16[64,2,128,32]{2,3,1,0:T(8,128)(2,1)}), bf16[64,2,128,32]{2,3,1,0:T(8,128)(2,1)}, u32[]{:S(2)}, u32[]{:S(2)}) async-start(bf16[64,2,128,32]{2,3,1,0:T(8,128)(2,1)} %get-tuple-element.24), calls=%async_computation.1 | async-start | bytes 2097152 | tf_op jit(solution)/shard_map/all_to_all | solution.py:25
  109.0 1.2 copy-start.1
  111.3 60.9 %all-to-all-start.2 = ((bf16[64,2,128,32]{2,3,1,0:T(8,128)(2,1)}), bf16[64,2,128,32]{2,3,1,0:T(8,128)(2,1)}, u32[]{:S(2)}, u32[]{:S(2)}) async-start(bf16[64,2,128,32]{2,3,1,0:T(8,128)(2,1)} %get-tuple-element.6), calls=%async_computation.2 | async-start | bytes 2097152 | tf_op jit(solution)/shard_map/all_to_all | solution.py:25
  118.8 107.8 %all-gather.3.cloned.1.call-start = ((), (), s32[]{:S(2)}) async-start(), calls=%async_computation.6 | async-start | bytes 1179648 | tf_op jit(solution)/shard_map/all_gather | solution.py:85
  175.3 14.8 %copy-start.3 = (s32[1024]{0:T(1024)S(1)}, s32[1024]{0:T(1024)}, u32[]{:S(2)}) copy-start(s32[1024]{0:T(1024)} %param.13) | copy-start | bytes 12292
  194.6 23.0 %all-to-all-start.3 = ((f32[64,1,512]{2,1,0:T(1,128)}), f32[64,1,512]{2,1,0:T(1,128)S(1)}, u32[]{:S(2)}, u32[]{:S(2)}) async-start(f32[64,1,512]{2,1,0:T(1,128)} %reshape.211), calls=%async_computation.3 | async-start | bytes 262144 | tf_op jit(solution)/shard_map/all_to_all | solution.py:25
  220.2 21.7 %all-to-all-start.4 = ((f32[64,1,512]{2,1,0:T(1,128)}), f32[64,1,512]{2,1,0:T(1,128)S(1)}, u32[]{:S(2)}, u32[]{:S(2)}) async-start(f32[64,1,512]{2,1,0:T(1,128)} %reshape.213), calls=%async_computation.4 | async-start | bytes 262144 | tf_op jit(solution)/shard_map/all_to_all | solution.py:11
  241.9 107.8 %all-to-all-start.5 = ((bf16[64,2,128,64]{2,1,3,0:T(2,128)(2,1)}), bf16[64,2,128,64]{2,1,3,0:T(2,128)(2,1)}, u32[]{:S(2)}, u32[]{:S(2)}) async-start(bf16[64,2,128,64]{2,1,3,0:T(2,128)(2,1)} %copy.74), calls=%async_computation.5 | async-start | bytes 4194304 | tf_op jit(solution)/shard_map/all_to_all | solution.py:25
Sparse Core Ops, SparseCore 0:
  191.3 22.9 all-gather.2
